TPU v7x, 128 devices: a whole 4x4x4 slice. The times are simulated.
128 devices in a mesh: fsdp: 32 (over z, x, core), tensor: 4 (over y).
Axes of the slice: x: 4, y: 4, z: 4, core: 2. Of those that a mesh axis runs over, the one named last changes fastest.
Arguments:
- hidden: bfloat16 [512, 28672], P('tensor', 'fsdp'), may hold values from -6 to 6
- down_weight: bfloat16 [28672, 16384], P('fsdp', 'tensor'), may hold values from -0.03125 to 0.03125
- covariance: float32 [16384, 16384], P('tensor', 'fsdp'), as said below
- keep_index: int32 [32, 8], P('fsdp'), may hold values from -1 to 15, as said below
- start_basis: float32 [16384, 512], P('fsdp'), may hold values from -6 to 6
Outputs:
- mlp_out: bfloat16 [512, 16384], P('fsdp', 'tensor')
- new_covariance: float32 [16384, 16384], P('tensor', 'fsdp')
- first_basis: float32 [16384, 512], P(('tensor', 'fsdp'))
- final_basis: float32 [16384, 512], P('fsdp')
Inputs may be any that keep to these rules, and one draw needn't show every extreme that they name: `keep_index`: row b lists first between 1 and 8 distinct positions of 0 to 15, then -1 in the remaining slots; in every draw some row lists 8 positions. covariance is exactly symmetric and positive definite.
All inputs are finite; a program needn't handle non-finite values.
Results may differ from a plain program's by a relative error of at most 0.0015.
Values may be sent and summed in bfloat16 or wider, within the bound.
A program may use at most 128 MiB of HBM per device.

v0:
```python
import math
import jax
import jax.numpy as jnp
from jax import lax
from jax.sharding import PartitionSpec as P

D = 16384
TOK_DEV = 16


def broadcast(x, axis, root):
    mine = lax.axis_index(axis) == root
    return lax.psum(jnp.where(mine, x, jnp.zeros_like(x)), axis)


def gram_local(image_rows):
    return jnp.dot(
        image_rows.T,
        image_rows,
        precision=lax.Precision.HIGHEST,
        preferred_element_type=jnp.float32,
    )


def solve_rows(image_rows, lower_factor):
    return jax.scipy.linalg.solve_triangular(lower_factor, image_rows.T, lower=True).T


def body(hidden, down_weight, covariance, keep_index, start_basis):
    highest = lax.Precision.HIGHEST
    fsdp_count = lax.axis_size("fsdp")
    total_tokens = TOK_DEV * fsdp_count
    quarter = covariance.shape[0]
    block_width = covariance.shape[1]
    share_rows = quarter // fsdp_count
    group_size = fsdp_count // lax.axis_size("tensor")
    all_hidden = lax.all_gather(hidden, "tensor", axis=0, tiled=True)
    mlp_out = lax.psum_scatter(
        jnp.dot(all_hidden, down_weight, preferred_element_type=jnp.float32),
        "fsdp",
        scatter_dimension=0,
        tiled=True,
    ).astype(jnp.bfloat16)
    listed = keep_index[0]
    fsdp_index = lax.axis_index("fsdp")
    col_offset = fsdp_index % group_size * block_width
    source_index = fsdp_index // group_size
    positions = jnp.arange(mlp_out.shape[0], dtype=jnp.int32)
    marked = jnp.any(listed[:, None] == positions[None, :], axis=0).astype(jnp.bfloat16)
    row_data = lax.all_gather(mlp_out * marked[:, None], "fsdp", axis=0, tiled=True)
    column_data = broadcast(
        lax.dynamic_slice_in_dim(row_data, col_offset, block_width, 1), "tensor", source_index
    )
    update = lax.dot_general(
        row_data, column_data, (((0,), (0,)), ((), ())), preferred_element_type=jnp.float32
    )
    new_covariance = covariance + update * (1.0 / total_tokens)
    partial_image = jnp.dot(
        new_covariance, start_basis, precision=highest, preferred_element_type=jnp.float32
    )
    first_image = lax.psum(partial_image, "fsdp")
    first_gram = lax.psum(gram_local(first_image), "tensor")
    own_image = lax.dynamic_slice_in_dim(first_image, fsdp_index * share_rows, share_rows, 0)
    first_factor = jnp.linalg.cholesky(first_gram)
    first_basis = solve_rows(own_image, first_factor) * math.sqrt(D)
    carried = solve_rows(first_image, first_factor)
    partial_second = lax.dot_general(
        new_covariance,
        carried,
        (((0,), (0,)), ((), ())),
        precision=highest,
        preferred_element_type=jnp.float32,
    )
    second = lax.psum(partial_second, "tensor")
    second_gram = lax.psum(gram_local(second), "fsdp")
    final_basis = solve_rows(second, jnp.linalg.cholesky(second_gram)) * math.sqrt(D)
    return (mlp_out, new_covariance, first_basis, final_basis)


def solution(mesh):
    placed = (
        P("tensor", "fsdp"),
        P("fsdp", "tensor"),
        P("tensor", "fsdp"),
        P("fsdp", None),
        P("fsdp", None),
    )
    return jax.shard_map(
        body,
        mesh=mesh,
        in_specs=placed,
        out_specs=(
            P("fsdp", "tensor"),
            P("tensor", "fsdp"),
            P(("tensor", "fsdp"), None),
            P("fsdp", None),
        ),
        check_vma=False,
    )
```

profile of v0, /device:TPU:1, one launch (start us, length us, event | category | flops | bytes accessed | tf_op | source)
XLA Modules:
  0.0 948.6 jit_solution(741812926708005223)
XLA Ops:
  7.2 14.1 %all_gather.6 = bf16[512,896]{1,0:T(8,128)(2,1)S(1)} all-gather(bf16[128,896]{1,0:T(8,128)(2,1)} %param.6), channel_id=1, replica_groups=mesh['fsdp'=32,'tensor'=4] {'tensor'}, dimensions={0}, use_global_device_ids=true | all-gather | bytes 1146880 | tf_op jit(solution)/shard_map/all_gather | solution.py:37
  21.3 9.8 %fusion.96 = f32[512,4096]{1,0:T(8,128)} fusion(bf16[512,896]{1,0:T(8,128)(2,1)S(1)} %all_gather.6, bf16[896,4096]{1,0:T(8,128)(2,1)} %param.7), kind=kOutput, calls=%fused_computation.169 | convolution fusion | flops 3758096384 | bytes 16646144 | tf_op jit(solution)/shard_map/dot_general | solution.py:39
  31.8 94.6 %reduce-scatter.2.cloned.1.call-done = f32[16,4096]{1,0:T(8,128)} async-done(((f32[512,4096]{1,0:T(8,128)}), f32[16,4096]{1,0:T(8,128)}) %reduce-scatter.2.cloned.1.call-update) | async-done | bytes 262160 | tf_op jit(solution)/shard_map/reduce_scatter | solution.py:38
  128.2 48.6 %all-gather.2.cloned.1.call-done = bf16[512,4096]{1,0:T(8,128)(2,1)} async-done(((bf16[16,4096]{1,0:T(8,128)(2,1)}), bf16[512,4096]{1,0:T(8,128)(2,1)}) %all-gather.2.cloned.1.call-update) | async-done | bytes 4194320 | tf_op jit(solution)/shard_map/all_gather | solution.py:50
  178.8 40.7 %all-reduce.7.cloned.1.call-done = bf16[512,512]{1,0:T(8,128)(2,1)} async-done(((bf16[512,512]{1,0:T(8,128)(2,1)}), bf16[512,512]{1,0:T(8,128)(2,1)}) %all-reduce.7.cloned.1.call-update) | async-done | bytes 524304 | tf_op jit(solution)/shard_map/psum | solution.py:13
  230.3 15.7 %fusion.97 = f32[4096,512]{1,0:T(8,128)} fusion(f32[4096,512]{1,0:T(8,128)S(1)} %multiply_add_fusion, f32[512,512]{1,0:T(8,128)S(1)} %copy-done), kind=kOutput, calls=%fused_computation.170 | convolution fusion | flops 12884901888 | bytes 17825792 | tf_op jit(solution)/shard_map/dot_general | solution.py:58
  246.4 122.9 %all-reduce.9.cloned.1.call-done = f32[4096,512]{1,0:T(8,128)} async-done(((f32[4096,512]{1,0:T(8,128)}), f32[4096,512]{1,0:T(8,128)}) %all-reduce.9.cloned.1.call-update) | async-done | bytes 8388624 | tf_op jit(solution)/shard_map/psum | solution.py:61
  369.2 18.5 %fusion.98 = f32[512,512]{0,1:T(8,128)} fusion(f32[4096,512]{1,0:T(8,128)} %all-reduce.9.cloned.1.call-done), kind=kOutput, calls=%fused_computation.171 | convolution fusion | flops 12884901888 | bytes 9437184 | tf_op jit(solution)/shard_map/dot_general | solution.py:17
  388.8 43.1 %all-reduce.11.cloned.1.call-done = f32[512,512]{0,1:T(8,128)} async-done(((f32[512,512]{0,1:T(8,128)}), f32[512,512]{0,1:T(8,128)}) %all-reduce.11.cloned.1.call-update) | async-done | bytes 1048592 | tf_op jit(solution)/shard_map/psum | solution.py:62
  434.9 11.7 %cholesky.286 = f32[128,128]{1,0:T(8,128)S(1)} custom-call(f32[128,128]{1,0:T(8,128)S(1)} %cholesky.426), custom_call_target="Cholesky" | custom-call | tf_op jit(solution)/shard_map/jit(cholesky)/cholesky | solution.py:64
  446.8 9.8 %custom-call.36 = f32[1,128,128]{1,2,0:T(8,128)S(1)} custom-call(f32[1,128,128]{2,1,0:T(8,128)S(1)} %get-tuple-element.70), custom_call_target="InvertDiagBlocksLowerTriangular" | custom-call | tf_op jit(solution)/shard_map/jit(cholesky)/cholesky | solution.py:64
  457.3 11.7 %cholesky.305 = f32[128,128]{1,0:T(8,128)S(1)} custom-call(f32[128,128]{1,0:T(8,128)S(1)} %cholesky.430), custom_call_target="Cholesky" | custom-call | tf_op jit(solution)/shard_map/jit(cholesky)/cholesky | solution.py:64
  469.0 18.5 %custom-call.37 = f32[1,128,128]{1,2,0:T(8,128)S(1)} custom-call(f32[1,128,128]{2,1,0:T(8,128)S(1)} %get-tuple-element.67), custom_call_target="InvertDiagBlocksLowerTriangular" | custom-call | tf_op jit(solution)/shard_map/jit(cholesky)/cholesky | solution.py:64
  488.2 11.7 %cholesky.326 = f32[128,128]{1,0:T(8,128)S(1)} custom-call(f32[128,128]{1,0:T(8,128)S(1)} %cholesky.435), custom_call_target="Cholesky" | custom-call | tf_op jit(solution)/shard_map/jit(cholesky)/cholesky | solution.py:64
  500.0 9.8 %custom-call.38 = f32[1,128,128]{1,2,0:T(8,128)S(1)} custom-call(f32[1,128,128]{2,1,0:T(8,128)S(1)} %get-tuple-element.64), custom_call_target="InvertDiagBlocksLowerTriangular" | custom-call | tf_op jit(solution)/shard_map/jit(cholesky)/cholesky | solution.py:64
  510.4 11.7 %cholesky.343 = f32[128,128]{1,0:T(8,128)S(1)} custom-call(f32[128,128]{1,0:T(8,128)S(1)} %convolution_subtract_fusion.13), custom_call_target="Cholesky" | custom-call | tf_op jit(solution)/shard_map/jit(cholesky)/cholesky | solution.py:64
  527.1 8.0 while.2
  535.1 39.3 %custom-call.31 = f32[4,128,128]{1,2,0:T(8,128)S(1)} custom-call(f32[4,128,128]{2,1,0:T(8,128)S(1)} %get-tuple-element.12), custom_call_target="InvertDiagBlocksLowerTriangular" | custom-call | tf_op jit(solution)/shard_map/jit(_solve_triangular)/triangular_solve | solution.py:26
  585.0 8.9 convolution_subtract_fusion
  595.9 12.4 %fusion.14 = f32[128,4096]{0,1:T(8,128)S(1)} fusion(f32[128,4096]{1,0:T(8,128)S(1)} %fusion.80, f32[128,4096]{1,0:T(8,128)S(1)} %fusion.78, f32[128,4096]{1,0:T(8,128)S(1)} %fusion.20, f32[512,4096]{0,1:T(8,128)} %bitcast.127, f32[512,512]{1,0:T(8,128)S(1)} %get-tuple-element.179), kind=kOutput, calls=%fused_computation.21 | convolution fusion | flops 2419589120 | bytes 10682368 | tf_op jit(solution)/shard_map/jit(_solve_triangular)/triangular_solve | solution.py:26
  610.3 29.5 %fusion = f32[512,512]{1,0:T(8,128)} fusion(f32[4096,512]{1,0:T(8,128)S(1)} %bitcast.129, f32[128,4096]{1,0:T(8,128)S(1)} %fusion.82, f32[128,4096]{1,0:T(8,128)S(1)} %fusion.80, f32[128,4096]{1,0:T(8,128)S(1)} %fusion.78, f32[128,4096]{1,0:T(8,128)S(1)} %fusion.20), kind=kOutput, calls=%fused_computation.4 | convolution fusion | flops 12891193344 | bytes 17825792 | tf_op jit(solution)/shard_map/dot_general | solution.py:67
  641.5 45.5 %all-reduce.13.cloned.1.call-done = f32[512,512]{1,0:T(8,128)} async-done(((f32[512,512]{1,0:T(8,128)}), f32[512,512]{1,0:T(8,128)}) %all-reduce.13.cloned.1.call-update) | async-done | bytes 1048592 | tf_op jit(solution)/shard_map/psum | solution.py:74
  693.1 106.8 %all-reduce.15.cloned.1.call-done = f32[512,512]{0,1:T(8,128)} async-done(((f32[512,512]{0,1:T(8,128)}), f32[512,512]{0,1:T(8,128)}) %all-reduce.15.cloned.1.call-update) | async-done | bytes 1048592 | tf_op jit(solution)/shard_map/psum | solution.py:75
  802.9 11.7 %cholesky.358 = f32[128,128]{1,0:T(8,128)S(1)} custom-call(f32[128,128]{1,0:T(8,128)S(1)} %cholesky.439), custom_call_target="Cholesky" | custom-call | tf_op jit(solution)/shard_map/jit(cholesky)/cholesky | solution.py:76
  814.8 9.8 %custom-call.39 = f32[1,128,128]{1,2,0:T(8,128)S(1)} custom-call(f32[1,128,128]{2,1,0:T(8,128)S(1)} %get-tuple-element.60), custom_call_target="InvertDiagBlocksLowerTriangular" | custom-call | tf_op jit(solution)/shard_map/jit(cholesky)/cholesky | solution.py:76
  825.3 11.9 %cholesky.377 = f32[128,128]{1,0:T(8,128)S(1)} custom-call(f32[128,128]{1,0:T(8,128)S(1)} %cholesky.443), custom_call_target="Cholesky" | custom-call | tf_op jit(solution)/shard_map/jit(cholesky)/cholesky | solution.py:76
  837.2 9.8 %custom-call.40 = f32[1,128,128]{1,2,0:T(8,128)S(1)} custom-call(f32[1,128,128]{2,1,0:T(8,128)S(1)} %get-tuple-element.57), custom_call_target="InvertDiagBlocksLowerTriangular" | custom-call | tf_op jit(solution)/shard_map/jit(cholesky)/cholesky | solution.py:76
  847.7 11.7 %cholesky.398 = f32[128,128]{1,0:T(8,128)S(1)} custom-call(f32[128,128]{1,0:T(8,128)S(1)} %cholesky.448), custom_call_target="Cholesky" | custom-call | tf_op jit(solution)/shard_map/jit(cholesky)/cholesky | solution.py:76
  859.5 9.8 %custom-call.41 = f32[1,128,128]{1,2,0:T(8,128)S(1)} custom-call(f32[1,128,128]{2,1,0:T(8,128)S(1)} %get-tuple-element.54), custom_call_target="InvertDiagBlocksLowerTriangular" | custom-call | tf_op jit(solution)/shard_map/jit(cholesky)/cholesky | solution.py:76
  869.9 11.9 %cholesky.415 = f32[128,128]{1,0:T(8,128)S(1)} custom-call(f32[128,128]{1,0:T(8,128)S(1)} %convolution_subtract_fusion.11), custom_call_target="Cholesky" | custom-call | tf_op jit(solution)/shard_map/jit(cholesky)/cholesky | solution.py:76
  887.2 8.5 while.3
  895.7 39.3 %custom-call.32 = f32[4,128,128]{1,2,0:T(8,128)S(1)} custom-call(f32[4,128,128]{2,1,0:T(8,128)S(1)} %get-tuple-element.20), custom_call_target="InvertDiagBlocksLowerTriangular" | custom-call | tf_op jit(solution)/shard_map/jit(_solve_triangular)/triangular_solve | solution.py:26
  (128 shorter events, 76.9 us)
Async XLA Ops:
  7.2 223.2 %copy-start = (f32[512,512]{1,0:T(8,128)S(1)}, f32[512,512]{1,0:T(8,128)}, u32[]{:S(2)}) copy-start(f32[512,512]{1,0:T(8,128)} %param.10) | copy-start | bytes 3145732
  7.2 119.2 %reduce-scatter.2.cloned.1.call-start = ((), (), s32[]{:S(2)}) async-start(), calls=%async_computation.1 | async-start | bytes 8650752 | tf_op jit(solution)/shard_map/reduce_scatter | solution.py:38
  31.1 0.7 copy-start.4
  31.1 145.6 %all-gather.2.cloned.1.call-start = ((), (), s32[]{:S(2)}) async-start(), calls=%async_computation.2 | async-start | bytes 4325376 | tf_op jit(solution)/shard_map/all_gather | solution.py:50
  128.1 91.4 %all-reduce.7.cloned.1.call-start = ((), (), s32[]{:S(2)}) async-start(), calls=%async_computation.3 | async-start | bytes 1048576 | tf_op jit(solution)/shard_map/psum | solution.py:13
  178.7 190.5 %all-reduce.9.cloned.1.call-start = ((), (), s32[]{:S(2)}) async-start(), calls=%async_computation.4 | async-start | bytes 16777216 | tf_op jit(solution)/shard_map/psum | solution.py:61
  226.9 3.4 copy-start.2
  246.1 185.8 %all-reduce.11.cloned.1.call-start = ((), (), s32[]{:S(2)}) async-start(), calls=%async_computation.5 | async-start | bytes 2097152 | tf_op jit(solution)/shard_map/psum | solution.py:62
  387.7 299.3 %all-reduce.13.cloned.1.call-start = ((), (), s32[]{:S(2)}) async-start(), calls=%async_computation.6 | async-start | bytes 2097152 | tf_op jit(solution)/shard_map/psum | solution.py:74
  593.9 16.4 %slice-start = ((s8[8388608]{0:T(1024)(128)(4,1)}), s8[4194304]{0:T(1024)(128)(4,1)S(1)}, s32[]{:S(2)}) async-start(s8[8388608]{0:T(1024)(128)(4,1)} %bitcast.128), calls=%async_computation.8 | async-start | bytes 8388608
  595.9 14.4 %slice-start.1 = ((s8[8388608]{0:T(1024)(128)(4,1)}), s8[4194304]{0:T(1024)(128)(4,1)S(1)}, s32[]{:S(2)}) async-start(s8[8388608]{0:T(1024)(128)(4,1)} %bitcast.128), calls=%async_computation.9 | async-start | bytes 8388608
  639.9 160.0 %all-reduce.15.cloned.1.call-start = ((), (), s32[]{:S(2)}) async-start(), calls=%async_computation.7 | async-start | bytes 2097152 | tf_op jit(solution)/shard_map/psum | solution.py:75
  802.9 132.1 %copy-start.3 = (f32[512,512]{1,0:T(8,128)S(1)}, f32[512,512]{1,0:T(8,128)}, u32[]{:S(2)}) copy-start(f32[512,512]{1,0:T(8,128)} %all-reduce.13.cloned.1.call-done) | copy-start | bytes 3145732
  935.5 5.8 copy-start.1
Sparse Core Ops, SparseCore 0:
  31.2 95.1 reduce-scatter.1
  129.2 47.4 all-gather.1
  179.7 39.7 all-reduce.6
  246.2 122.9 all-reduce.8
  387.9 43.9 all-reduce.10
  640.0 46.9 all-reduce.12
  691.5 108.3 all-reduce.14
where the time goes:
time: 957 us; the launch traced here: 949 us
  waiting for transfers between devices  502 us (52%)
  other arithmetic  253 us (26%)
  matrix products  132 us (14%)
  local copies, waits for them, and re-layouts  26.9 us (3%)
  between operations  20.2 us (2%)
  blocking collectives  14.1 us (1%)
    psum x1, waiting for transfers between devices, body(): first_image = lax.psum(partial_image, 'fsdp')  123 us
    psum x1, waiting for transfers between devices, body(): second_gram = lax.psum(gram_local(second), 'fsdp')  107 us
    reduce_scatter x1, waiting for transfers between devices, body(): lax.psum_scatter(jnp.dot(all_hidden, down_weight, preferred_element_type=...  94.6 us
    another operation x14, other arithmetic, body(): first_factor = jnp.linalg.cholesky(first_gram)  87 us
    another operation x15, other arithmetic, body(): jnp.linalg.cholesky(second_gram)  79.5 us
    another operation x5, other arithmetic, solve_rows(): jax.scipy.linalg.solve_triangular(lower_factor, image_rows.T, lower=True)  79.3 us
    all_gather x1, waiting for transfers between devices, body(): lax.all_gather(mlp_out * marked[:, None], 'fsdp', axis=0, tiled=True)  48.6 us
    psum x1, waiting for transfers between devices, body(): second = lax.psum(partial_second, 'tensor')  45.5 us
  transfers between devices with their start and end apart: 7, of which 7 were waited for; matrix products, arithmetic and copies ran while one was open for 0% of the time, Pallas kernels for 0%

commit v1 on v0

--- a/solution.py
+++ b/solution.py
@@ -1,11 +1,21 @@
+import functools
 import math
 import jax
 import jax.numpy as jnp
 from jax import lax
 from jax.sharding import PartitionSpec as P
+from jax.lax import all_to_all, axis_size
 
 D = 16384
 TOK_DEV = 16
+
+
+def _convert_links(tile_in, link_axis):
+    even = jnp.stack([tile_in for _ in range(axis_size(link_axis))], axis=0)
+    return jnp.concatenate(all_to_all(even, link_axis, 0, 0), 0)
+
+
+part_set = functools.partial(_convert_links, link_axis="fsdp")
 
 
 def broadcast(x, axis, root):
@@ -47,7 +57,7 @@
     source_index = fsdp_index // group_size
     positions = jnp.arange(mlp_out.shape[0], dtype=jnp.int32)
     marked = jnp.any(listed[:, None] == positions[None, :], axis=0).astype(jnp.bfloat16)
-    row_data = lax.all_gather(mlp_out * marked[:, None], "fsdp", axis=0, tiled=True)
+    row_data = part_set(mlp_out * marked[:, None])
     column_data = broadcast(
         lax.dynamic_slice_in_dim(row_data, col_offset, block_width, 1), "tensor", source_index
     )

time: 957 us -> 955 us (level)
    all_to_all x0 -> x1, waiting for transfers between devices: none -> 50.6 us  [_convert_links(): return jnp.concatenate(all_to_all(even, link_axis, 0, 0), 0)]
    all_gather x1 -> x0, waiting for transfers between devices: 48.6 us -> none  [body(): lax.all_gather(mlp_out * marked[:, None], 'fsdp', axis=0, tiled=True)]
where the time goes in v1:
time: 955 us; the launch traced here: 951 us
  waiting for transfers between devices  504 us (53%)
  other arithmetic  244 us (26%)
  matrix products  132 us (14%)
  local copies, waits for them, and re-layouts  29.1 us (3%)
  between operations  20.1 us (2%)
  blocking collectives  14.1 us (1%)
    psum x1, waiting for transfers between devices, body(): first_image = lax.psum(partial_image, 'fsdp')  123 us
    psum x1, waiting for transfers between devices, body(): second_gram = lax.psum(gram_local(second), 'fsdp')  107 us
    reduce_scatter x1, waiting for transfers between devices, body(): lax.psum_scatter(jnp.dot(all_hidden, down_weight, preferred_element_type=...  94.5 us
    another operation x15, other arithmetic, body(): jnp.linalg.cholesky(second_gram)  79.5 us
    another operation x5, other arithmetic, solve_rows(): jax.scipy.linalg.solve_triangular(lower_factor, image_rows.T, lower=True)  79.3 us
    another operation x14, other arithmetic, body(): first_factor = jnp.linalg.cholesky(first_gram)  78.5 us
    all_to_all x1, waiting for transfers between devices, _convert_links(): return jnp.concatenate(all_to_all(even, link_axis, 0, 0), 0)  50.6 us
    psum x1, waiting for transfers between devices, body(): second = lax.psum(partial_second, 'tensor')  45.6 us
  transfers between devices with their start and end apart: 7, of which 7 were waited for; matrix products, arithmetic and copies ran while one was open for 0% of the time, Pallas kernels for 0%

profile of v1, /device:TPU:1, one launch (start us, length us, event | category | flops | bytes accessed | tf_op | source)
XLA Modules:
  0.0 951.2 jit_solution(8934179416089410934)
XLA Ops:
  7.2 14.1 %all_gather.3 = bf16[512,896]{1,0:T(8,128)(2,1)S(1)} all-gather(bf16[128,896]{1,0:T(8,128)(2,1)} %param.6), channel_id=1, replica_groups=mesh['fsdp'=32,'tensor'=4] {'tensor'}, dimensions={0}, use_global_device_ids=true | all-gather | bytes 1146880 | tf_op jit(solution)/shard_map/all_gather | solution.py:47
  21.3 9.8 %fusion.96 = f32[512,4096]{1,0:T(8,128)} fusion(bf16[512,896]{1,0:T(8,128)(2,1)S(1)} %all_gather.3, bf16[896,4096]{1,0:T(8,128)(2,1)} %param.7), kind=kOutput, calls=%fused_computation.169 | convolution fusion | flops 3758096384 | bytes 16646144 | tf_op jit(solution)/shard_map/dot_general | solution.py:49
  31.8 94.5 %reduce-scatter.2.cloned.1.call-done = f32[16,4096]{1,0:T(8,128)} async-done(((f32[512,4096]{1,0:T(8,128)}), f32[16,4096]{1,0:T(8,128)}) %reduce-scatter.2.cloned.1.call-update) | async-done | bytes 262160 | tf_op jit(solution)/shard_map/reduce_scatter | solution.py:48
  138.0 50.6 %all-to-all-done = bf16[32,16,4096]{2,1,0:T(8,128)(2,1)} async-done(((bf16[32,16,4096]{2,1,0:T(8,128)(2,1)}), bf16[32,16,4096]{2,1,0:T(8,128)(2,1)}, u32[]{:S(2)}, u32[]{:S(2)}) %all-to-all-start) | async-done | bytes 4194336 | tf_op jit(solution)/shard_map/all_to_all | solution.py:15
  190.8 40.2 %all-reduce.7.cloned.1.call-done = bf16[512,512]{1,0:T(8,128)(2,1)} async-done(((bf16[512,512]{1,0:T(8,128)(2,1)}), bf16[512,512]{1,0:T(8,128)(2,1)}) %all-reduce.7.cloned.1.call-update) | async-done | bytes 524304 | tf_op jit(solution)/shard_map/psum | solution.py:23
  241.9 15.7 %fusion.97 = f32[4096,512]{1,0:T(8,128)} fusion(f32[4096,512]{1,0:T(8,128)S(1)} %multiply_add_fusion, f32[512,512]{1,0:T(8,128)S(1)} %copy-done), kind=kOutput, calls=%fused_computation.170 | convolution fusion | flops 12884901888 | bytes 17825792 | tf_op jit(solution)/shard_map/dot_general | solution.py:68
  258.1 122.6 %all-reduce.9.cloned.1.call-done = f32[4096,512]{1,0:T(8,128)} async-done(((f32[4096,512]{1,0:T(8,128)}), f32[4096,512]{1,0:T(8,128)}) %all-reduce.9.cloned.1.call-update) | async-done | bytes 8388624 | tf_op jit(solution)/shard_map/psum | solution.py:71
  380.7 18.5 %fusion.98 = f32[512,512]{0,1:T(8,128)} fusion(f32[4096,512]{1,0:T(8,128)} %all-reduce.9.cloned.1.call-done), kind=kOutput, calls=%fused_computation.171 | convolution fusion | flops 12884901888 | bytes 9437184 | tf_op jit(solution)/shard_map/dot_general | solution.py:27
  400.3 43.1 %all-reduce.11.cloned.1.call-done = f32[512,512]{0,1:T(8,128)} async-done(((f32[512,512]{0,1:T(8,128)}), f32[512,512]{0,1:T(8,128)}) %all-reduce.11.cloned.1.call-update) | async-done | bytes 1048592 | tf_op jit(solution)/shard_map/psum | solution.py:72
  446.4 11.7 %cholesky.286 = f32[128,128]{1,0:T(8,128)S(1)} custom-call(f32[128,128]{1,0:T(8,128)S(1)} %cholesky.426), custom_call_target="Cholesky" | custom-call | tf_op jit(solution)/shard_map/jit(cholesky)/cholesky | solution.py:74
  458.3 9.8 %custom-call.36 = f32[1,128,128]{1,2,0:T(8,128)S(1)} custom-call(f32[1,128,128]{2,1,0:T(8,128)S(1)} %get-tuple-element.70), custom_call_target="InvertDiagBlocksLowerTriangular" | custom-call | tf_op jit(solution)/shard_map/jit(cholesky)/cholesky | solution.py:74
  468.8 11.7 %cholesky.305 = f32[128,128]{1,0:T(8,128)S(1)} custom-call(f32[128,128]{1,0:T(8,128)S(1)} %cholesky.430), custom_call_target="Cholesky" | custom-call | tf_op jit(solution)/shard_map/jit(cholesky)/cholesky | solution.py:74
  480.5 10.0 %custom-call.37 = f32[1,128,128]{1,2,0:T(8,128)S(1)} custom-call(f32[1,128,128]{2,1,0:T(8,128)S(1)} %get-tuple-element.67), custom_call_target="InvertDiagBlocksLowerTriangular" | custom-call | tf_op jit(solution)/shard_map/jit(cholesky)/cholesky | solution.py:74
  491.1 11.7 %cholesky.326 = f32[128,128]{1,0:T(8,128)S(1)} custom-call(f32[128,128]{1,0:T(8,128)S(1)} %cholesky.435), custom_call_target="Cholesky" | custom-call | tf_op jit(solution)/shard_map/jit(cholesky)/cholesky | solution.py:74
  502.9 9.8 %custom-call.38 = f32[1,128,128]{1,2,0:T(8,128)S(1)} custom-call(f32[1,128,128]{2,1,0:T(8,128)S(1)} %get-tuple-element.64), custom_call_target="InvertDiagBlocksLowerTriangular" | custom-call | tf_op jit(solution)/shard_map/jit(cholesky)/cholesky | solution.py:74
  513.3 11.7 %cholesky.343 = f32[128,128]{1,0:T(8,128)S(1)} custom-call(f32[128,128]{1,0:T(8,128)S(1)} %convolution_subtract_fusion.13), custom_call_target="Cholesky" | custom-call | tf_op jit(solution)/shard_map/jit(cholesky)/cholesky | solution.py:74
  530.0 7.7 while.2
  537.7 39.3 %custom-call.31 = f32[4,128,128]{1,2,0:T(8,128)S(1)} custom-call(f32[4,128,128]{2,1,0:T(8,128)S(1)} %get-tuple-element.12), custom_call_target="InvertDiagBlocksLowerTriangular" | custom-call | tf_op jit(solution)/shard_map/jit(_solve_triangular)/triangular_solve | solution.py:36
  587.6 8.9 convolution_subtract_fusion
  598.5 12.4 %fusion.14 = f32[128,4096]{0,1:T(8,128)S(1)} fusion(f32[128,4096]{1,0:T(8,128)S(1)} %fusion.80, f32[128,4096]{1,0:T(8,128)S(1)} %fusion.78, f32[128,4096]{1,0:T(8,128)S(1)} %fusion.20, f32[512,4096]{0,1:T(8,128)} %bitcast.128, f32[512,512]{1,0:T(8,128)S(1)} %get-tuple-element.179), kind=kOutput, calls=%fused_computation.21 | convolution fusion | flops 2419589120 | bytes 10682368 | tf_op jit(solution)/shard_map/jit(_solve_triangular)/triangular_solve | solution.py:36
  612.9 29.5 %fusion = f32[512,512]{1,0:T(8,128)} fusion(f32[4096,512]{1,0:T(8,128)S(1)} %bitcast.130, f32[128,4096]{1,0:T(8,128)S(1)} %fusion.82, f32[128,4096]{1,0:T(8,128)S(1)} %fusion.80, f32[128,4096]{1,0:T(8,128)S(1)} %fusion.78, f32[128,4096]{1,0:T(8,128)S(1)} %fusion.20), kind=kOutput, calls=%fused_computation.4 | convolution fusion | flops 12891193344 | bytes 17825792 | tf_op jit(solution)/shard_map/dot_general | solution.py:77
  644.0 45.6 %all-reduce.13.cloned.1.call-done = f32[512,512]{1,0:T(8,128)} async-done(((f32[512,512]{1,0:T(8,128)}), f32[512,512]{1,0:T(8,128)}) %all-reduce.13.cloned.1.call-update) | async-done | bytes 1048592 | tf_op jit(solution)/shard_map/psum | solution.py:84
  695.7 106.8 %all-reduce.15.cloned.1.call-done = f32[512,512]{0,1:T(8,128)} async-done(((f32[512,512]{0,1:T(8,128)}), f32[512,512]{0,1:T(8,128)}) %all-reduce.15.cloned.1.call-update) | async-done | bytes 1048592 | tf_op jit(solution)/shard_map/psum | solution.py:85
  805.5 11.7 %cholesky.358 = f32[128,128]{1,0:T(8,128)S(1)} custom-call(f32[128,128]{1,0:T(8,128)S(1)} %cholesky.439), custom_call_target="Cholesky" | custom-call | tf_op jit(solution)/shard_map/jit(cholesky)/cholesky | solution.py:86
  817.4 9.8 %custom-call.39 = f32[1,128,128]{1,2,0:T(8,128)S(1)} custom-call(f32[1,128,128]{2,1,0:T(8,128)S(1)} %get-tuple-element.60), custom_call_target="InvertDiagBlocksLowerTriangular" | custom-call | tf_op jit(solution)/shard_map/jit(cholesky)/cholesky | solution.py:86
  827.9 11.9 %cholesky.377 = f32[128,128]{1,0:T(8,128)S(1)} custom-call(f32[128,128]{1,0:T(8,128)S(1)} %cholesky.443), custom_call_target="Cholesky" | custom-call | tf_op jit(solution)/shard_map/jit(cholesky)/cholesky | solution.py:86
  839.8 9.8 %custom-call.40 = f32[1,128,128]{1,2,0:T(8,128)S(1)} custom-call(f32[1,128,128]{2,1,0:T(8,128)S(1)} %get-tuple-element.57), custom_call_target="InvertDiagBlocksLowerTriangular" | custom-call | tf_op jit(solution)/shard_map/jit(cholesky)/cholesky | solution.py:86
  850.3 11.7 %cholesky.398 = f32[128,128]{1,0:T(8,128)S(1)} custom-call(f32[128,128]{1,0:T(8,128)S(1)} %cholesky.448), custom_call_target="Cholesky" | custom-call | tf_op jit(solution)/shard_map/jit(cholesky)/cholesky | solution.py:86
  862.1 9.8 %custom-call.41 = f32[1,128,128]{1,2,0:T(8,128)S(1)} custom-call(f32[1,128,128]{2,1,0:T(8,128)S(1)} %get-tuple-element.54), custom_call_target="InvertDiagBlocksLowerTriangular" | custom-call | tf_op jit(solution)/shard_map/jit(cholesky)/cholesky | solution.py:86
  872.5 11.9 %cholesky.415 = f32[128,128]{1,0:T(8,128)S(1)} custom-call(f32[128,128]{1,0:T(8,128)S(1)} %convolution_subtract_fusion.11), custom_call_target="Cholesky" | custom-call | tf_op jit(solution)/shard_map/jit(cholesky)/cholesky | solution.py:86
  889.8 8.5 while.3
  898.3 39.3 %custom-call.32 = f32[4,128,128]{1,2,0:T(8,128)S(1)} custom-call(f32[4,128,128]{2,1,0:T(8,128)S(1)} %get-tuple-element.20), custom_call_target="InvertDiagBlocksLowerTriangular" | custom-call | tf_op jit(solution)/shard_map/jit(_solve_triangular)/triangular_solve | solution.py:36
  (128 shorter events, 86.9 us)
Async XLA Ops:
  7.2 234.7 %copy-start = (f32[512,512]{1,0:T(8,128)S(1)}, f32[512,512]{1,0:T(8,128)}, u32[]{:S(2)}) copy-start(f32[512,512]{1,0:T(8,128)} %param.10) | copy-start | bytes 3145732
  7.2 119.2 %reduce-scatter.2.cloned.1.call-start = ((), (), s32[]{:S(2)}) async-start(), calls=%async_computation.2 | async-start | bytes 8650752 | tf_op jit(solution)/shard_map/reduce_scatter | solution.py:48
  31.1 0.7 copy-start.4
  130.5 58.1 %all-to-all-start = ((bf16[32,16,4096]{2,1,0:T(8,128)(2,1)}), bf16[32,16,4096]{2,1,0:T(8,128)(2,1)}, u32[]{:S(2)}, u32[]{:S(2)}) async-start(bf16[32,16,4096]{2,1,0:T(8,128)(2,1)} %stack.2), calls=%async_computation.1 | async-start | bytes 8388608 | tf_op jit(solution)/shard_map/all_to_all | solution.py:15
  138.0 93.1 %all-reduce.7.cloned.1.call-start = ((), (), s32[]{:S(2)}) async-start(), calls=%async_computation.3 | async-start | bytes 1048576 | tf_op jit(solution)/shard_map/psum | solution.py:23
  190.6 190.1 %all-reduce.9.cloned.1.call-start = ((), (), s32[]{:S(2)}) async-start(), calls=%async_computation.4 | async-start | bytes 16777216 | tf_op jit(solution)/shard_map/psum | solution.py:71
  238.5 3.4 copy-start.2
  257.6 185.8 %all-reduce.11.cloned.1.call-start = ((), (), s32[]{:S(2)}) async-start(), calls=%async_computation.5 | async-start | bytes 2097152 | tf_op jit(solution)/shard_map/psum | solution.py:72
  399.2 290.4 %all-reduce.13.cloned.1.call-start = ((), (), s32[]{:S(2)}) async-start(), calls=%async_computation.6 | async-start | bytes 2097152 | tf_op jit(solution)/shard_map/psum | solution.py:84
  596.5 16.4 %slice-start = ((s8[8388608]{0:T(1024)(128)(4,1)}), s8[4194304]{0:T(1024)(128)(4,1)S(1)}, s32[]{:S(2)}) async-start(s8[8388608]{0:T(1024)(128)(4,1)} %bitcast.129), calls=%async_computation.8 | async-start | bytes 8388608
  598.5 14.4 %slice-start.1 = ((s8[8388608]{0:T(1024)(128)(4,1)}), s8[4194304]{0:T(1024)(128)(4,1)S(1)}, s32[]{:S(2)}) async-start(s8[8388608]{0:T(1024)(128)(4,1)} %bitcast.129), calls=%async_computation.9 | async-start | bytes 8388608
  642.4 160.1 %all-reduce.15.cloned.1.call-start = ((), (), s32[]{:S(2)}) async-start(), calls=%async_computation.7 | async-start | bytes 2097152 | tf_op jit(solution)/shard_map/psum | solution.py:85
  805.5 132.1 %copy-start.3 = (f32[512,512]{1,0:T(8,128)S(1)}, f32[512,512]{1,0:T(8,128)}, u32[]{:S(2)}) copy-start(f32[512,512]{1,0:T(8,128)} %all-reduce.13.cloned.1.call-done) | copy-start | bytes 3145732
  938.1 5.8 copy-start.1
Sparse Core Ops, SparseCore 0:
  31.2 95.0 reduce-scatter.1
  190.7 40.2 all-reduce.6
  257.7 122.9 all-reduce.8
  399.4 43.9 all-reduce.10
  642.6 47.0 all-reduce.12
  694.1 108.3 all-reduce.14
